TPU v7x, 512 devices: a whole 4x4x16 slice. The times are simulated.
512 devices in a mesh: tx: 8 (over x, core), ty: 16 (over z), tz: 4 (over y).
Axes of the slice: x: 4, y: 4, z: 16, core: 2. Of those that a mesh axis runs over, the one named last changes fastest.
Arguments:
- start_block: float32 [64, 1048576], P(None, ('tx', 'ty', 'tz'))
- weights: bfloat16 [8192, 6, 128, 128], P(('tx', 'ty', 'tz')), may hold values from 0 to 0.25, as said below
- neighbours: int32 [8192, 6], P(('tx', 'ty', 'tz')), may hold values from 0 to 123, as said below
- boundary: int32 [2048], P(('tx', 'ty', 'tz')), may hold values from 0 to 15, as said below
Outputs:
- basis: float32 [64, 1048576], P(None, ('tx', 'ty', 'tz'))
- rfactor: float32 [64, 64], replicated
Inputs may be any that keep to these rules, and one draw needn't show every extreme that they name: `neighbours`: slot 0 of block row b is b % 16; in the last of each device's 16 rows slot 1 is 123. `boundary`: each device's 4 entries are distinct, the last of them 16 - 1. For each block row b and point p, exactly 16 of the entries weights[b, s, q, p] over all slots s and rows q are nonzero, each positive.
All inputs are finite; a program needn't handle non-finite values.
Results may differ from a plain program's by a relative error of at most 0.00075.
Values may be sent and summed in bfloat16 or wider, within the bound.
No kernel may reach another device: no remote copies, remote signals or barrier semaphores. Data moves between devices by JAX's collectives and lax.ppermute only.
A program may use at most 64 MiB of HBM per device.

v0:
```python
import jax
import jax.numpy as jnp
from jax import lax
from jax.sharding import PartitionSpec as P


def extended(block, sides, width):
    for axis, dim in sides:
        count = lax.axis_size(axis)
        forward = [(i, i + 1) for i in range(count - 1)]
        backward = [(target, source) for source, target in forward]
        low = lax.ppermute(
            lax.slice_in_dim(block, block.shape[dim] - width, None, axis=dim), axis, forward
        )
        high = lax.ppermute(lax.slice_in_dim(block, 0, width, axis=dim), axis, backward)
        block = jnp.concatenate([low, block, high], axis=dim)
    return block


def take_edges(grid, boundary):
    return jnp.take(grid, boundary, axis=1)[:, None, None, None]


def boundary_halo(edge_part):
    return extended(edge_part, (("tx", 1), ("ty", 2), ("tz", 3)), 1)


def as_pool(haloed):
    return haloed.reshape(haloed.shape[0], -1, haloed.shape[-1])


def apply_operator(current, own_grid, far_grid, degree, weights, neighbours):
    pool_grid = jnp.concatenate([own_grid, far_grid], axis=1)
    picked = jnp.take(pool_grid, neighbours, axis=1)
    product = jnp.einsum("kisq,isqp->kip", picked, weights, preferred_element_type=jnp.float32)
    return current * (1.0 - degree * 0.125) + product.reshape(current.shape) * 0.125


def lower_factor(mixed):
    local_gram = jnp.dot(
        mixed, mixed.T, precision=lax.Precision.HIGHEST, preferred_element_type=jnp.float32
    )
    total = lax.psum(local_gram, ("tx", "ty", "tz"))
    return jnp.linalg.cholesky(total)


def solve_lower(lower, values):
    return lax.linalg.triangular_solve(lower, values, left_side=True, lower=True)


def per_device(start_block, weights, neighbours, boundary):
    width, points = start_block.shape
    block_size = weights.shape[-1]
    blocks = points // block_size
    devices = lax.axis_size("tx") * lax.axis_size("ty") * lax.axis_size("tz")
    root_scale = float(points * devices) ** 0.5
    degree = jnp.sum(weights, axis=(1, 2), dtype=jnp.float32).reshape(points)
    own_grid = start_block.astype(jnp.bfloat16).reshape(width, blocks, block_size)
    far_grid = as_pool(boundary_halo(take_edges(own_grid, boundary)))
    mixed = apply_operator(start_block, own_grid, far_grid, degree, weights, neighbours)
    lower = lower_factor(mixed)
    current = solve_lower(lower, mixed) * root_scale
    own_grid = current.astype(jnp.bfloat16).reshape(width, blocks, block_size)
    far_grid = as_pool(boundary_halo(take_edges(own_grid, boundary)))
    mixed = apply_operator(current, own_grid, far_grid, degree, weights, neighbours)
    lower = lower_factor(mixed)
    basis = solve_lower(lower, mixed) * root_scale
    return (basis, lower.T / root_scale)


def solution(mesh):
    placed = (
        P(None, ("tx", "ty", "tz")),
        P(("tx", "ty", "tz"), None, None, None),
        P(("tx", "ty", "tz"), None),
        P(("tx", "ty", "tz")),
    )
    return jax.shard_map(
        per_device,
        mesh=mesh,
        in_specs=placed,
        out_specs=(P(None, ("tx", "ty", "tz")), P()),
        check_vma=False,
    )
```

profile of v0, /device:TPU:1, one launch (start us, length us, event | category | flops | bytes accessed | tf_op | source)
XLA Modules:
  0.0 328.7 jit_solution(997474695390738293)
XLA Ops:
  0.6 0.7 compare_and_fusion.1
  1.3 0.7 compare_select_fusion.1
  2.0 1.1 copy_bitcast_fusion.1
  3.1 0.6 gather_fusion
  3.7 8.8 %collective-permute-start.1 = (bf16[64,1,1,1,4,128]{5,0,4,3,2,1:T(8,128)(2,1)S(1)}, bf16[64,1,1,1,4,128]{5,0,4,3,2,1:T(8,128)(2,1)S(1)}, u32[]{:S(2)}, u32[]{:S(2)}) collective-permute-start(bf16[64,1,1,1,4,128]{5,0,4,3,2,1:T(8,128)(2,1)S(1)} %select_bitcast_fusion.1), channel_id=1, source_target_pairs={{64,0},{128,64},{192,128},{256,192},{320,256},{384,320},{448,384},... | collective-permute-start | bytes 196616 | tf_op jit(solution)/shard_map/ppermute | solution.py:15
  12.5 1.9 collective-permute-start
  14.4 0.7 compare_and_fusion
  15.8 1.3 collective-permute-start.3
  17.1 4.0 %collective-permute-start.2 = (bf16[64,3,1,1,4,128]{5,0,4,3,2,1:T(8,128)(2,1)S(1)}, bf16[64,3,1,1,4,128]{5,0,4,3,2,1:T(8,128)(2,1)S(1)}, u32[]{:S(2)}, u32[]{:S(2)}) collective-permute-start(bf16[64,3,1,1,4,128]{5,0,4,3,2,1:T(8,128)(2,1)S(1)} %pad_maximum_fusion.6), channel_id=1, source_target_pairs={{0,4},{4,8},{8,12},{12,16},{16,20},{20,24},{24,28},{28,32},{32,36}... | collective-permute-start | bytes 589832 | tf_op jit(solution)/shard_map/ppermute | solution.py:12
  21.1 0.7 compare_select_fusion
  21.9 2.2 collective-permute-done.3
  24.1 0.9 collective-permute-done.2
  25.0 1.3 collective-permute-start.5
  26.3 4.0 %collective-permute-start.4 = (bf16[64,3,3,1,4,128]{5,0,4,3,2,1:T(8,128)(2,1)S(1)}, bf16[64,3,3,1,4,128]{5,0,4,3,2,1:T(8,128)(2,1)S(1)}, u32[]{:S(2)}, u32[]{:S(2)}) collective-permute-start(bf16[64,3,3,1,4,128]{5,0,4,3,2,1:T(8,128)(2,1)S(1)} %pad_maximum_fusion.4), channel_id=1, source_target_pairs={{0,1},{1,2},{2,3},{4,5},{5,6},{6,7},{8,9},{9,10},{10,11},{12,13},{... | collective-permute-start | bytes 1769480 | tf_op jit(solution)/shard_map/ppermute | solution.py:12
  30.4 2.4 convert_reduce_fusion
  32.8 7.8 %collective-permute-done.5 = bf16[64,3,3,1,4,128]{5,0,4,3,2,1:T(8,128)(2,1)S(1)} collective-permute-done((bf16[64,3,3,1,4,128]{5,0,4,3,2,1:T(8,128)(2,1)S(1)}, bf16[64,3,3,1,4,128]{5,0,4,3,2,1:T(8,128)(2,1)S(1)}, u32[]{:S(2)}, u32[]{:S(2)}) %collective-permute-start.5) | collective-permute-done | bytes 589856 | tf_op jit(solution)/shard_map/ppermute | solution.py:15
  40.6 0.9 collective-permute-done.4
  41.9 2.0 gather_fusion.1
  43.9 3.2 fusion.23
  47.0 0.6 fusion.30
  47.6 108.8 %psum.14 = f32[64,64]{0,1:T(8,128)S(1)} all-reduce(f32[64,64]{0,1:T(8,128)S(1)} %fusion.30), channel_id=1, replica_groups=mesh['tx'=8,'ty'=16,'tz'=4] {'tx','ty','tz'}, use_global_device_ids=true, to_apply=%region_1.4 | all-reduce | flops 4096 | bytes 32768 | tf_op jit(solution)/shard_map/psum | solution.py:43
  156.5 5.8 %cholesky.44 = f32[64,64]{1,0:T(8,128)S(1)} custom-call(f32[64,64]{1,0:T(8,128)S(1)} %fusion.36), custom_call_target="Cholesky" | custom-call | tf_op jit(solution)/shard_map/jit(cholesky)/cholesky | solution.py:44
  162.4 0.6 compare_reduce_fusion.1
  163.1 0.7 fusion.32
  163.7 4.9 %custom-call.6 = f32[1,64,64]{1,2,0:T(8,128)S(1)} custom-call(f32[1,64,64]{2,1,0:T(8,128)S(1)} %fusion.32), custom_call_target="InvertDiagBlocksLowerTriangular" | custom-call | tf_op jit(solution)/shard_map/triangular_solve/custom-call.0 | solution.py:48
  168.6 0.6 fusion.29
  169.3 0.6 gather_fusion.2
  170.0 2.6 collective-permute-start.7
  172.6 3.0 collective-permute-start.6
  175.6 1.3 collective-permute-done.6
  176.9 1.3 collective-permute-start.9
  178.2 4.3 %collective-permute-start.8 = (bf16[64,3,1,1,4,128]{5,0,4,3,2,1:T(8,128)(2,1)S(1)}, bf16[64,3,1,1,4,128]{5,0,4,3,2,1:T(8,128)(2,1)S(1)}, u32[]{:S(2)}, u32[]{:S(2)}) collective-permute-start(bf16[64,3,1,1,4,128]{5,0,4,3,2,1:T(8,128)(2,1)S(1)} %pad_maximum_fusion.7), channel_id=1, source_target_pairs={{0,4},{4,8},{8,12},{12,16},{16,20},{20,24},{24,28},{28,32},{32,36}... | collective-permute-start | bytes 589832 | tf_op jit(solution)/shard_map/ppermute | solution.py:12
  182.4 2.4 collective-permute-done.9
  184.9 1.8 collective-permute-done.8
  186.7 1.3 collective-permute-start.11
  188.0 4.0 %collective-permute-start.10 = (bf16[64,3,3,1,4,128]{5,0,4,3,2,1:T(8,128)(2,1)S(1)}, bf16[64,3,3,1,4,128]{5,0,4,3,2,1:T(8,128)(2,1)S(1)}, u32[]{:S(2)}, u32[]{:S(2)}) collective-permute-start(bf16[64,3,3,1,4,128]{5,0,4,3,2,1:T(8,128)(2,1)S(1)} %pad_maximum_fusion.5), channel_id=1, source_target_pairs={{0,1},{1,2},{2,3},{4,5},{5,6},{6,7},{8,9},{9,10},{10,11},{12,13},{... | collective-permute-start | bytes 1769480 | tf_op jit(solution)/shard_map/ppermute | solution.py:12
  192.0 11.6 %collective-permute-done.11 = bf16[64,3,3,1,4,128]{5,0,4,3,2,1:T(8,128)(2,1)S(1)} collective-permute-done((bf16[64,3,3,1,4,128]{5,0,4,3,2,1:T(8,128)(2,1)S(1)}, bf16[64,3,3,1,4,128]{5,0,4,3,2,1:T(8,128)(2,1)S(1)}, u32[]{:S(2)}, u32[]{:S(2)}) %collective-permute-start.11) | collective-permute-done | bytes 589856 | tf_op jit(solution)/shard_map/ppermute | solution.py:15
  203.6 0.9 collective-permute-done.10
  204.9 2.0 gather_fusion.3
  206.9 3.1 fusion.17
  210.0 0.6 fusion.31
  210.5 103.8 %psum.15 = f32[64,64]{0,1:T(8,128)S(1)} all-reduce(f32[64,64]{0,1:T(8,128)S(1)} %fusion.31), channel_id=1, replica_groups=mesh['tx'=8,'ty'=16,'tz'=4] {'tx','ty','tz'}, use_global_device_ids=true, to_apply=%region_4.9 | all-reduce | flops 4096 | bytes 32768 | tf_op jit(solution)/shard_map/psum | solution.py:43
  314.5 5.8 %cholesky.55 = f32[64,64]{1,0:T(8,128)S(1)} custom-call(f32[64,64]{1,0:T(8,128)S(1)} %fusion.34), custom_call_target="Cholesky" | custom-call | tf_op jit(solution)/shard_map/jit(cholesky)/cholesky | solution.py:44
  320.4 0.6 compare_reduce_fusion
  321.0 0.7 multiply_bitcast_fusion
  321.7 0.7 copy.42
  322.4 4.9 %custom-call.7 = f32[1,64,64]{1,2,0:T(8,128)S(1)} custom-call(f32[1,64,64]{2,1,0:T(8,128)S(1)} %get-tuple-element.13), custom_call_target="InvertDiagBlocksLowerTriangular" | custom-call | tf_op jit(solution)/shard_map/triangular_solve/custom-call.0 | solution.py:48
  327.3 1.4 convolution_multiply_fusion
  (29 shorter events, 2.3 us)
Async XLA Ops:
  3.7 11.5 %collective-permute-start.1 = (bf16[64,1,1,1,4,128]{5,0,4,3,2,1:T(8,128)(2,1)S(1)}, bf16[64,1,1,1,4,128]{5,0,4,3,2,1:T(8,128)(2,1)S(1)}, u32[]{:S(2)}, u32[]{:S(2)}) collective-permute-start(bf16[64,1,1,1,4,128]{5,0,4,3,2,1:T(8,128)(2,1)S(1)} %select_bitcast_fusion.1), channel_id=1, source_target_pairs={{64,0},{128,64},{192,128},{256,192},{320,256},{384,320},{448,384},... | collective-permute-start | bytes 196616 | tf_op jit(solution)/shard_map/ppermute | solution.py:15
  12.5 3.2 collective-permute-start
  15.8 8.3 %collective-permute-start.3 = (bf16[64,3,1,1,4,128]{5,0,4,3,2,1:T(8,128)(2,1)S(1)}, bf16[64,3,1,1,4,128]{5,0,4,3,2,1:T(8,128)(2,1)S(1)}, u32[]{:S(2)}, u32[]{:S(2)}) collective-permute-start(bf16[64,3,1,1,4,128]{5,0,4,3,2,1:T(8,128)(2,1)S(1)} %pad_maximum_fusion.6), channel_id=1, source_target_pairs={{4,0},{8,4},{12,8},{16,12},{20,16},{24,20},{28,24},{32,28},{36,32}... | collective-permute-start | bytes 589832 | tf_op jit(solution)/shard_map/ppermute | solution.py:15
  17.1 7.9 %collective-permute-start.2 = (bf16[64,3,1,1,4,128]{5,0,4,3,2,1:T(8,128)(2,1)S(1)}, bf16[64,3,1,1,4,128]{5,0,4,3,2,1:T(8,128)(2,1)S(1)}, u32[]{:S(2)}, u32[]{:S(2)}) collective-permute-start(bf16[64,3,1,1,4,128]{5,0,4,3,2,1:T(8,128)(2,1)S(1)} %pad_maximum_fusion.6), channel_id=1, source_target_pairs={{0,4},{4,8},{8,12},{12,16},{16,20},{20,24},{24,28},{28,32},{32,36}... | collective-permute-start | bytes 589832 | tf_op jit(solution)/shard_map/ppermute | solution.py:12
  25.0 15.5 %collective-permute-start.5 = (bf16[64,3,3,1,4,128]{5,0,4,3,2,1:T(8,128)(2,1)S(1)}, bf16[64,3,3,1,4,128]{5,0,4,3,2,1:T(8,128)(2,1)S(1)}, u32[]{:S(2)}, u32[]{:S(2)}) collective-permute-start(bf16[64,3,3,1,4,128]{5,0,4,3,2,1:T(8,128)(2,1)S(1)} %pad_maximum_fusion.4), channel_id=1, source_target_pairs={{1,0},{2,1},{3,2},{5,4},{6,5},{7,6},{9,8},{10,9},{11,10},{13,12},{... | collective-permute-start | bytes 1769480 | tf_op jit(solution)/shard_map/ppermute | solution.py:15
  26.3 15.1 %collective-permute-start.4 = (bf16[64,3,3,1,4,128]{5,0,4,3,2,1:T(8,128)(2,1)S(1)}, bf16[64,3,3,1,4,128]{5,0,4,3,2,1:T(8,128)(2,1)S(1)}, u32[]{:S(2)}, u32[]{:S(2)}) collective-permute-start(bf16[64,3,3,1,4,128]{5,0,4,3,2,1:T(8,128)(2,1)S(1)} %pad_maximum_fusion.4), channel_id=1, source_target_pairs={{0,1},{1,2},{2,3},{4,5},{5,6},{6,7},{8,9},{9,10},{10,11},{12,13},{... | collective-permute-start | bytes 1769480 | tf_op jit(solution)/shard_map/ppermute | solution.py:12
  43.9 3.2 copy-start
  170.0 5.6 %collective-permute-start.7 = (bf16[64,1,1,1,4,128]{5,0,4,3,2,1:T(8,128)(2,1)S(1)}, bf16[64,1,1,1,4,128]{5,0,4,3,2,1:T(8,128)(2,1)S(1)}, u32[]{:S(2)}, u32[]{:S(2)}) collective-permute-start(bf16[64,1,1,1,4,128]{5,0,4,3,2,1:T(8,128)(2,1)S(1)} %select_bitcast_fusion), channel_id=1, source_target_pairs={{64,0},{128,64},{192,128},{256,192},{320,256},{384,320},{448,384},... | collective-permute-start | bytes 196616 | tf_op jit(solution)/shard_map/ppermute | solution.py:15
  172.6 4.3 %collective-permute-start.6 = (bf16[64,1,1,1,4,128]{5,0,4,3,2,1:T(8,128)(2,1)S(1)}, bf16[64,1,1,1,4,128]{5,0,4,3,2,1:T(8,128)(2,1)S(1)}, u32[]{:S(2)}, u32[]{:S(2)}) collective-permute-start(bf16[64,1,1,1,4,128]{5,0,4,3,2,1:T(8,128)(2,1)S(1)} %select_bitcast_fusion), channel_id=1, source_target_pairs={{0,64},{64,128},{128,192},{192,256},{256,320},{320,384},{384,448},... | collective-permute-start | bytes 196616 | tf_op jit(solution)/shard_map/ppermute | solution.py:12
  176.9 8.0 %collective-permute-start.9 = (bf16[64,3,1,1,4,128]{5,0,4,3,2,1:T(8,128)(2,1)S(1)}, bf16[64,3,1,1,4,128]{5,0,4,3,2,1:T(8,128)(2,1)S(1)}, u32[]{:S(2)}, u32[]{:S(2)}) collective-permute-start(bf16[64,3,1,1,4,128]{5,0,4,3,2,1:T(8,128)(2,1)S(1)} %pad_maximum_fusion.7), channel_id=1, source_target_pairs={{4,0},{8,4},{12,8},{16,12},{20,16},{24,20},{28,24},{32,28},{36,32}... | collective-permute-start | bytes 589832 | tf_op jit(solution)/shard_map/ppermute | solution.py:15
  178.2 8.4 %collective-permute-start.8 = (bf16[64,3,1,1,4,128]{5,0,4,3,2,1:T(8,128)(2,1)S(1)}, bf16[64,3,1,1,4,128]{5,0,4,3,2,1:T(8,128)(2,1)S(1)}, u32[]{:S(2)}, u32[]{:S(2)}) collective-permute-start(bf16[64,3,1,1,4,128]{5,0,4,3,2,1:T(8,128)(2,1)S(1)} %pad_maximum_fusion.7), channel_id=1, source_target_pairs={{0,4},{4,8},{8,12},{12,16},{16,20},{20,24},{24,28},{28,32},{32,36}... | collective-permute-start | bytes 589832 | tf_op jit(solution)/shard_map/ppermute | solution.py:12
  186.7 16.9 %collective-permute-start.11 = (bf16[64,3,3,1,4,128]{5,0,4,3,2,1:T(8,128)(2,1)S(1)}, bf16[64,3,3,1,4,128]{5,0,4,3,2,1:T(8,128)(2,1)S(1)}, u32[]{:S(2)}, u32[]{:S(2)}) collective-permute-start(bf16[64,3,3,1,4,128]{5,0,4,3,2,1:T(8,128)(2,1)S(1)} %pad_maximum_fusion.5), channel_id=1, source_target_pairs={{1,0},{2,1},{3,2},{5,4},{6,5},{7,6},{9,8},{10,9},{11,10},{13,12},{... | collective-permute-start | bytes 1769480 | tf_op jit(solution)/shard_map/ppermute | solution.py:15
  188.0 16.5 %collective-permute-start.10 = (bf16[64,3,3,1,4,128]{5,0,4,3,2,1:T(8,128)(2,1)S(1)}, bf16[64,3,3,1,4,128]{5,0,4,3,2,1:T(8,128)(2,1)S(1)}, u32[]{:S(2)}, u32[]{:S(2)}) collective-permute-start(bf16[64,3,3,1,4,128]{5,0,4,3,2,1:T(8,128)(2,1)S(1)} %pad_maximum_fusion.5), channel_id=1, source_target_pairs={{0,1},{1,2},{2,3},{4,5},{5,6},{6,7},{8,9},{9,10},{10,11},{12,13},{... | collective-permute-start | bytes 1769480 | tf_op jit(solution)/shard_map/ppermute | solution.py:12
where the time goes:
time: 330 us; the launch traced here: 329 us
  blocking collectives  213 us (65%)
  starting transfers between devices  37.7 us (11%)
  other arithmetic  31.6 us (10%)
  waiting for transfers between devices  30.1 us (9%)
  matrix products  9.49 us (3%)
  local copies, waits for them, and re-layouts  6.16 us (2%)
    psum x2, blocking collectives, lower_factor(): total = lax.psum(local_gram, ('tx', 'ty', 'tz'))  213 us
    ppermute x6, waiting for transfers between devices, extended(): lax.ppermute(lax.slice_in_dim(block, 0, width, axis=dim), axis, backward)  23.9 us
    ppermute x6, starting transfers between devices, extended(): lax.ppermute(lax.slice_in_dim(block, block.shape[dim] - width, None, axis...  21.2 us
    ppermute x6, starting transfers between devices, extended(): lax.ppermute(lax.slice_in_dim(block, 0, width, axis=dim), axis, backward)  16.5 us
    another operation x6, other arithmetic, lower_factor(): return jnp.linalg.cholesky(total)  13 us
    another operation x3, other arithmetic, solve_lower(): lax.linalg.triangular_solve(lower, values, left_side=True, lower=True)  10.4 us
  transfers between devices with their start and end apart: 12, of which 10 were waited for; matrix products, arithmetic and copies ran while one was open for 1% of the time, Pallas kernels for 0%

commit v1 on v0

--- a/solution.py
+++ b/solution.py
@@ -40,7 +40,7 @@
     local_gram = jnp.dot(
         mixed, mixed.T, precision=lax.Precision.HIGHEST, preferred_element_type=jnp.float32
     )
-    total = lax.psum(local_gram, ("tx", "ty", "tz"))
+    total = jnp.sum(lax.all_gather(local_gram, ("tx", "ty", "tz")), axis=0)
     return jnp.linalg.cholesky(total)
 
 

time: 330 us -> 588 us (1.78)
  waiting for transfers between devices: 30.1 us -> 473 us
  blocking collectives: 213 us -> 0 us
  other arithmetic: 31.6 us -> 45.5 us
  between operations: 0.93 us -> 14.3 us
    all_gather x0 -> x2, waiting for transfers between devices: none -> 443 us  [lower_factor(): total = jnp.sum(lax.all_gather(local_gram, ('tx', 'ty', 'tz')), axis=0)]
    psum x2 -> x0, blocking collectives: 213 us -> none  [lower_factor(): total = lax.psum(local_gram, ('tx', 'ty', 'tz'))]
    reduce_sum x0 -> x2, other arithmetic: none -> 13.9 us  [lower_factor(): total = jnp.sum(lax.all_gather(local_gram, ('tx', 'ty', 'tz')), axis=0)]
  transfers between devices with their start and end apart: 12 -> 14, of which waited for: 10 -> 12; matrix products, arithmetic and copies ran while one was open for 1% -> 1% of each run, Pallas kernels for 0% -> 0%
where the time goes in v1:
time: 588 us; the launch traced here: 587 us
  waiting for transfers between devices  473 us (80%)
  other arithmetic  45.5 us (8%)
  starting transfers between devices  37.7 us (6%)
  between operations  14.3 us (2%)
  matrix products  10.7 us (2%)
  local copies, waits for them, and re-layouts  6.16 us (1%)
    all_gather x2, waiting for transfers between devices, lower_factor(): total = jnp.sum(lax.all_gather(local_gram, ('tx', 'ty', 'tz')), axis=0)  443 us
    ppermute x6, waiting for transfers between devices, extended(): lax.ppermute(lax.slice_in_dim(block, 0, width, axis=dim), axis, backward)  23.7 us
    ppermute x6, starting transfers between devices, extended(): lax.ppermute(lax.slice_in_dim(block, block.shape[dim] - width, None, axis...  21.6 us
    ppermute x6, starting transfers between devices, extended(): lax.ppermute(lax.slice_in_dim(block, 0, width, axis=dim), axis, backward)  16.1 us
    reduce_sum x2, other arithmetic, lower_factor(): total = jnp.sum(lax.all_gather(local_gram, ('tx', 'ty', 'tz')), axis=0)  13.9 us
    another operation x6, other arithmetic, lower_factor(): return jnp.linalg.cholesky(total)  13 us
  transfers between devices with their start and end apart: 14, of which 12 were waited for; matrix products, arithmetic and copies ran while one was open for 1% of the time, Pallas kernels for 0%

profile of v1, /device:TPU:1, one launch (start us, length us, event | category | flops | bytes accessed | tf_op | source)
XLA Modules:
  0.0 587.4 jit_solution(13456410168277262901)
XLA Ops:
  7.2 0.7 compare_and_fusion.1
  7.9 0.7 compare_select_fusion.1
  8.5 1.1 copy_bitcast_fusion.1
  10.3 8.8 %collective-permute-start.1 = (bf16[64,1,1,1,4,128]{5,0,4,3,2,1:T(8,128)(2,1)S(1)}, bf16[64,1,1,1,4,128]{5,0,4,3,2,1:T(8,128)(2,1)S(1)}, u32[]{:S(2)}, u32[]{:S(2)}) collective-permute-start(bf16[64,1,1,1,4,128]{5,0,4,3,2,1:T(8,128)(2,1)S(1)} %select_bitcast_fusion.1), channel_id=1, source_target_pairs={{64,0},{128,64},{192,128},{256,192},{320,256},{384,320},{448,384},... | collective-permute-start | bytes 196616 | tf_op jit(solution)/shard_map/ppermute | solution.py:15
  19.1 1.9 collective-permute-start
  21.0 0.7 compare_and_fusion
  22.3 1.3 collective-permute-start.3
  23.6 4.0 collective-permute-start.2
  27.6 0.7 compare_select_fusion
  28.5 2.2 collective-permute-done.3
  30.7 0.9 collective-permute-done.2
  31.6 1.3 collective-permute-start.5
  32.9 4.0 collective-permute-start.4
  37.0 2.4 convert_reduce_fusion
  39.4 7.8 %collective-permute-done.5 = bf16[64,3,3,1,4,128]{5,0,4,3,2,1:T(8,128)(2,1)S(1)} collective-permute-done((bf16[64,3,3,1,4,128]{5,0,4,3,2,1:T(8,128)(2,1)S(1)}, bf16[64,3,3,1,4,128]{5,0,4,3,2,1:T(8,128)(2,1)S(1)}, u32[]{:S(2)}, u32[]{:S(2)}) %collective-permute-start.5) | collective-permute-done | bytes 589856 | tf_op jit(solution)/shard_map/ppermute | solution.py:15
  47.2 0.9 collective-permute-done.4
  48.5 2.0 gather_fusion.1
  50.4 3.2 fusion.23
  53.6 1.2 fusion.30
  54.9 224.1 %all-gather.5.cloned.1.call-done = f32[32768,64]{1,0:T(8,128)} async-done(((f32[64,64]{1,0:T(8,128)}), f32[32768,64]{1,0:T(8,128)}) %all-gather.5.cloned.1.call-update) | async-done | bytes 8388624 | tf_op jit(solution)/shard_map/all_gather | solution.py:43
  278.9 6.9 %reduce_sum.28 = f32[64,64]{1,0:T(8,128)S(1)} reduce(f32[512,64,64]{2,1,0:T(8,128)} %bitcast.96, f32[]{:T(128)} %constant.57.clone.1), dimensions={0}, to_apply=%region_1.4 | reduce | flops 2093056 | bytes 8404996 | tf_op jit(solution)/shard_map/reduce_sum | solution.py:43
  286.0 5.8 cholesky.44
  291.9 0.6 compare_reduce_fusion.1
  292.5 0.7 fusion.32
  293.2 4.9 custom-call.6
  298.1 0.7 fusion.29
  299.4 2.1 collective-permute-start.7
  301.6 3.4 collective-permute-start.6
  305.0 1.3 collective-permute-done.6
  306.3 1.3 collective-permute-start.9
  307.6 4.0 collective-permute-start.8
  311.6 2.2 collective-permute-done.9
  313.9 1.8 collective-permute-done.8
  315.7 1.3 collective-permute-start.11
  317.0 4.2 collective-permute-start.10
  321.2 11.5 %collective-permute-done.11 = bf16[64,3,3,1,4,128]{5,0,4,3,2,1:T(8,128)(2,1)S(1)} collective-permute-done((bf16[64,3,3,1,4,128]{5,0,4,3,2,1:T(8,128)(2,1)S(1)}, bf16[64,3,3,1,4,128]{5,0,4,3,2,1:T(8,128)(2,1)S(1)}, u32[]{:S(2)}, u32[]{:S(2)}) %collective-permute-start.11) | collective-permute-done | bytes 589856 | tf_op jit(solution)/shard_map/ppermute | solution.py:15
  332.7 1.0 collective-permute-done.10
  334.2 2.0 gather_fusion.3
  336.1 3.1 fusion.17
  339.2 1.2 fusion.31
  340.4 218.9 %all-gather.7.cloned.1.call-done = f32[32768,64]{1,0:T(8,128)} async-done(((f32[64,64]{1,0:T(8,128)}), f32[32768,64]{1,0:T(8,128)}) %all-gather.7.cloned.1.call-update) | async-done | bytes 8388624 | tf_op jit(solution)/shard_map/all_gather | solution.py:43
  559.3 6.9 %reduce_sum.29 = f32[64,64]{1,0:T(8,128)S(1)} reduce(f32[512,64,64]{2,1,0:T(8,128)} %bitcast.97, f32[]{:T(128)} %constant.57.clone.1), dimensions={0}, to_apply=%region_4.9 | reduce | flops 2093056 | bytes 8404996 | tf_op jit(solution)/shard_map/reduce_sum | solution.py:43
  566.3 5.8 cholesky.55
  572.2 0.6 compare_reduce_fusion
  572.9 0.7 multiply_bitcast_fusion
  573.5 0.7 copy.49
  574.2 4.9 custom-call.7
  579.1 1.4 convolution_multiply_fusion
  (35 shorter events, 3.5 us)
Async XLA Ops:
  7.2 271.8 %all-gather.5.cloned.1.call-start = ((), (), s32[]{:S(2)}) async-start(), calls=%async_computation | async-start | bytes 16809984 | tf_op jit(solution)/shard_map/all_gather | solution.py:43
  10.3 11.5 %collective-permute-start.1 = (bf16[64,1,1,1,4,128]{5,0,4,3,2,1:T(8,128)(2,1)S(1)}, bf16[64,1,1,1,4,128]{5,0,4,3,2,1:T(8,128)(2,1)S(1)}, u32[]{:S(2)}, u32[]{:S(2)}) collective-permute-start(bf16[64,1,1,1,4,128]{5,0,4,3,2,1:T(8,128)(2,1)S(1)} %select_bitcast_fusion.1), channel_id=1, source_target_pairs={{64,0},{128,64},{192,128},{256,192},{320,256},{384,320},{448,384},... | collective-permute-start | bytes 196616 | tf_op jit(solution)/shard_map/ppermute | solution.py:15
  19.1 3.2 collective-permute-start
  22.3 8.3 %collective-permute-start.3 = (bf16[64,3,1,1,4,128]{5,0,4,3,2,1:T(8,128)(2,1)S(1)}, bf16[64,3,1,1,4,128]{5,0,4,3,2,1:T(8,128)(2,1)S(1)}, u32[]{:S(2)}, u32[]{:S(2)}) collective-permute-start(bf16[64,3,1,1,4,128]{5,0,4,3,2,1:T(8,128)(2,1)S(1)} %pad_maximum_fusion.6), channel_id=1, source_target_pairs={{4,0},{8,4},{12,8},{16,12},{20,16},{24,20},{28,24},{32,28},{36,32}... | collective-permute-start | bytes 589832 | tf_op jit(solution)/shard_map/ppermute | solution.py:15
  23.6 7.9 %collective-permute-start.2 = (bf16[64,3,1,1,4,128]{5,0,4,3,2,1:T(8,128)(2,1)S(1)}, bf16[64,3,1,1,4,128]{5,0,4,3,2,1:T(8,128)(2,1)S(1)}, u32[]{:S(2)}, u32[]{:S(2)}) collective-permute-start(bf16[64,3,1,1,4,128]{5,0,4,3,2,1:T(8,128)(2,1)S(1)} %pad_maximum_fusion.6), channel_id=1, source_target_pairs={{0,4},{4,8},{8,12},{12,16},{16,20},{20,24},{24,28},{28,32},{32,36}... | collective-permute-start | bytes 589832 | tf_op jit(solution)/shard_map/ppermute | solution.py:12
  31.6 15.5 %collective-permute-start.5 = (bf16[64,3,3,1,4,128]{5,0,4,3,2,1:T(8,128)(2,1)S(1)}, bf16[64,3,3,1,4,128]{5,0,4,3,2,1:T(8,128)(2,1)S(1)}, u32[]{:S(2)}, u32[]{:S(2)}) collective-permute-start(bf16[64,3,3,1,4,128]{5,0,4,3,2,1:T(8,128)(2,1)S(1)} %pad_maximum_fusion.4), channel_id=1, source_target_pairs={{1,0},{2,1},{3,2},{5,4},{6,5},{7,6},{9,8},{10,9},{11,10},{13,12},{... | collective-permute-start | bytes 1769480 | tf_op jit(solution)/shard_map/ppermute | solution.py:15
  32.9 15.1 %collective-permute-start.4 = (bf16[64,3,3,1,4,128]{5,0,4,3,2,1:T(8,128)(2,1)S(1)}, bf16[64,3,3,1,4,128]{5,0,4,3,2,1:T(8,128)(2,1)S(1)}, u32[]{:S(2)}, u32[]{:S(2)}) collective-permute-start(bf16[64,3,3,1,4,128]{5,0,4,3,2,1:T(8,128)(2,1)S(1)} %pad_maximum_fusion.4), channel_id=1, source_target_pairs={{0,1},{1,2},{2,3},{4,5},{5,6},{6,7},{8,9},{9,10},{10,11},{12,13},{... | collective-permute-start | bytes 1769480 | tf_op jit(solution)/shard_map/ppermute | solution.py:12
  50.4 3.2 copy-start
  54.8 504.5 %all-gather.7.cloned.1.call-start = ((), (), s32[]{:S(2)}) async-start(), calls=%async_computation.1 | async-start | bytes 16809984 | tf_op jit(solution)/shard_map/all_gather | solution.py:43
  299.4 5.6 collective-permute-start.7
  301.6 4.7 collective-permute-start.6
  306.3 7.6 %collective-permute-start.9 = (bf16[64,3,1,1,4,128]{5,0,4,3,2,1:T(8,128)(2,1)S(1)}, bf16[64,3,1,1,4,128]{5,0,4,3,2,1:T(8,128)(2,1)S(1)}, u32[]{:S(2)}, u32[]{:S(2)}) collective-permute-start(bf16[64,3,1,1,4,128]{5,0,4,3,2,1:T(8,128)(2,1)S(1)} %pad_maximum_fusion.7), channel_id=1, source_target_pairs={{4,0},{8,4},{12,8},{16,12},{20,16},{24,20},{28,24},{32,28},{36,32}... | collective-permute-start | bytes 589832 | tf_op jit(solution)/shard_map/ppermute | solution.py:15
  307.6 8.0 %collective-permute-start.8 = (bf16[64,3,1,1,4,128]{5,0,4,3,2,1:T(8,128)(2,1)S(1)}, bf16[64,3,1,1,4,128]{5,0,4,3,2,1:T(8,128)(2,1)S(1)}, u32[]{:S(2)}, u32[]{:S(2)}) collective-permute-start(bf16[64,3,1,1,4,128]{5,0,4,3,2,1:T(8,128)(2,1)S(1)} %pad_maximum_fusion.7), channel_id=1, source_target_pairs={{0,4},{4,8},{8,12},{12,16},{16,20},{20,24},{24,28},{28,32},{32,36}... | collective-permute-start | bytes 589832 | tf_op jit(solution)/shard_map/ppermute | solution.py:12
  315.7 17.0 %collective-permute-start.11 = (bf16[64,3,3,1,4,128]{5,0,4,3,2,1:T(8,128)(2,1)S(1)}, bf16[64,3,3,1,4,128]{5,0,4,3,2,1:T(8,128)(2,1)S(1)}, u32[]{:S(2)}, u32[]{:S(2)}) collective-permute-start(bf16[64,3,3,1,4,128]{5,0,4,3,2,1:T(8,128)(2,1)S(1)} %pad_maximum_fusion.5), channel_id=1, source_target_pairs={{1,0},{2,1},{3,2},{5,4},{6,5},{7,6},{9,8},{10,9},{11,10},{13,12},{... | collective-permute-start | bytes 1769480 | tf_op jit(solution)/shard_map/ppermute | solution.py:15
  317.0 16.7 %collective-permute-start.10 = (bf16[64,3,3,1,4,128]{5,0,4,3,2,1:T(8,128)(2,1)S(1)}, bf16[64,3,3,1,4,128]{5,0,4,3,2,1:T(8,128)(2,1)S(1)}, u32[]{:S(2)}, u32[]{:S(2)}) collective-permute-start(bf16[64,3,3,1,4,128]{5,0,4,3,2,1:T(8,128)(2,1)S(1)} %pad_maximum_fusion.5), channel_id=1, source_target_pairs={{0,1},{1,2},{2,3},{4,5},{5,6},{6,7},{8,9},{9,10},{10,11},{12,13},{... | collective-permute-start | bytes 1769480 | tf_op jit(solution)/shard_map/ppermute | solution.py:12
Sparse Core Ops, SparseCore 0:
  55.0 223.9 all-gather.4
  340.5 218.7 all-gather.6
